TPU v7x, 32 devices: a whole 2x2x4 slice. The times are simulated.
32 devices in a mesh: lat: 8 (over z, y), lon: 4 (over x, core).
Axes of the slice: x: 2, y: 2, z: 4, core: 2. Of those that a mesh axis runs over, the one named last changes fastest.
Arguments:
- fields: bfloat16 [69, 128, 512], P(None, 'lat', 'lon'), may hold values from -6 to 6
- enc_kernel: bfloat16 [3, 3, 256, 69], replicated, may hold values from -0.25 to 0.25
- gen_kernel: bfloat16 [3, 3, 69, 256], replicated, may hold values from -0.125 to 0.125
- recon_grad: bfloat16 [69, 128, 512], P(None, 'lat', 'lon'), may hold values from -6 to 6
Outputs:
- rebuilt: bfloat16 [69, 128, 512], P(None, 'lat', 'lon')
- feat_grad: bfloat16 [256, 128, 512], P(None, 'lat', 'lon')
- enc_grad: float32 [3, 3, 256, 69], replicated
- gen_grad: float32 [3, 3, 69, 256], replicated
All inputs are finite; a program needn't handle non-finite values.
Results may differ from a plain program's by a relative error of at most 0.0085.
Values may be sent and summed in bfloat16 or wider, within the bound.
A program may use at most 64 MiB of HBM per device.

v0:
```python
import jax
import jax.numpy as jnp
from jax import lax
from jax.sharding import PartitionSpec as P


def extended(cells, sides, width, closed):
    for axis, dim in sides:
        count = lax.axis_size(axis)
        ends = count if closed else count - 1
        head = lax.slice_in_dim(cells, 0, width, axis=dim)
        tail = lax.slice_in_dim(cells, cells.shape[dim] - width, cells.shape[dim], axis=dim)
        cells = jnp.concatenate(
            [
                lax.ppermute(tail, axis, [(i, (i + 1) % count) for i in range(ends)]),
                cells,
                lax.ppermute(head, axis, [((i + 1) % count, i) for i in range(ends)]),
            ],
            axis=dim,
        )
    return cells


def from_behind(value, axis, steps):
    count = lax.axis_size(axis)
    pairs = [(source, (source + steps) % count) for source in range(count)]
    return lax.ppermute(value, axis, pairs)


def face_pad(source):
    lon_count = lax.axis_size("lon")
    widened = extended(source, (("lon", 2),), 1, True)
    edge_rows = jnp.concatenate([widened[:, :1], widened[:, -1:]], axis=1)
    pole_rows = from_behind(edge_rows, "lon", lon_count // 2)
    plain_pad = extended(widened, (("lat", 1),), 1, False)
    result = (plain_pad, pole_rows)
    return result


def with_poles(plain_pad, pole_rows):
    lat_index = lax.axis_index("lat")
    lat_count = lax.axis_size("lat")
    upper = jnp.where(lat_index == 0, pole_rows[:, :1], plain_pad[:, :1])
    lower = jnp.where(lat_index == lat_count - 1, pole_rows[:, 1:], plain_pad[:, -1:])
    return jnp.concatenate([upper, plain_pad[:, 1:-1], lower], axis=1)


def convolve(padded, kernel, height, width):
    running = None
    for row_tap in range(3):
        for col_tap in range(3):
            section = padded[:, row_tap : row_tap + height, col_tap : col_tap + width].reshape(
                padded.shape[0], height * width
            )
            product = jnp.dot(kernel[row_tap, col_tap], section, preferred_element_type=jnp.float32)
            running = product if running is None else running + product
    return running.reshape(kernel.shape[2], height, width)


def adjoint_conv(padded, kernel, height, width):
    running = None
    for row_tap in range(3):
        for col_tap in range(3):
            section = padded[
                :, 2 - row_tap : 2 - row_tap + height, 2 - col_tap : 2 - col_tap + width
            ].reshape(padded.shape[0], height * width)
            product = lax.dot_general(
                kernel[row_tap, col_tap],
                section,
                (((0,), (0,)), ((), ())),
                preferred_element_type=jnp.float32,
            )
            running = product if running is None else running + product
    return running.reshape(kernel.shape[3], height, width)


def pole_terms(pole_rows, kernel, width):
    terms = []
    for which, row_tap in ((0, 0), (1, 2)):
        running = None
        for col_tap in range(3):
            section = pole_rows[:, which, 2 - col_tap : 2 - col_tap + width]
            product = lax.dot_general(
                kernel[row_tap, col_tap],
                section,
                (((0,), (0,)), ((), ())),
                preferred_element_type=jnp.float32,
            )
            running = product if running is None else running + product
        terms.append(running)
    return (terms[0], terms[1])


def weight_grad(cotangent, padded, height, width):
    flat_cot = cotangent.reshape(cotangent.shape[0], height * width)
    taps = []
    for row_tap in range(3):
        row_list = []
        for col_tap in range(3):
            section = padded[:, row_tap : row_tap + height, col_tap : col_tap + width].reshape(
                padded.shape[0], height * width
            )
            row_list.append(
                lax.dot_general(
                    flat_cot, section, (((1,), (1,)), ((), ())), preferred_element_type=jnp.float32
                )
            )
        taps.append(jnp.stack(row_list))
    return jnp.stack(taps)


def sum_grads(enc_part, gen_part):
    summed = lax.psum((enc_part, gen_part), ("lat", "lon"))
    return summed


def on_device(fields, enc_kernel, gen_kernel, recon_grad):
    height = fields.shape[1]
    width = fields.shape[2]
    in_count = fields.shape[0]
    lat_index = lax.axis_index("lat")
    lat_count = lax.axis_size("lat")
    lon_count = lax.axis_size("lon")
    plain_pair, pole_pair = face_pad(jnp.concatenate([fields, recon_grad], axis=0))
    plain_in = plain_pair[:in_count]
    pole_in = pole_pair[:in_count]
    plain_cot = plain_pair[in_count:]
    pole_cot = pole_pair[in_count:]
    padded_in = with_poles(plain_in, pole_in)
    pre_act = convolve(padded_in, enc_kernel, height, width)
    hidden = jax.nn.silu(pre_act).astype(jnp.bfloat16)
    plain_hid, pole_hid = face_pad(hidden)
    padded_hid = with_poles(plain_hid, pole_hid)
    rebuilt = convolve(padded_hid, gen_kernel, height, width).astype(jnp.bfloat16)
    feat_f32 = adjoint_conv(plain_cot, gen_kernel, height, width)
    upper_term, lower_term = pole_terms(pole_cot, gen_kernel, width)
    feat_f32 = feat_f32.at[:, 0].add(jnp.where(lat_index == 0, upper_term, 0.0))
    feat_f32 = feat_f32.at[:, -1].add(jnp.where(lat_index == lat_count - 1, lower_term, 0.0))
    feat_grad = feat_f32.astype(jnp.bfloat16)
    logistic = jax.nn.sigmoid(pre_act)
    pre_grad = (
        feat_grad.astype(jnp.float32) * logistic * (1.0 + pre_act * (1.0 - logistic))
    ).astype(jnp.bfloat16)
    gen_part = weight_grad(recon_grad, padded_hid, height, width)
    enc_part = weight_grad(pre_grad, padded_in, height, width)
    enc_sum, gen_sum = sum_grads(enc_part, gen_part)
    norm_scale = 1.0 / jnp.sqrt(jnp.float32(height * lat_count * width * lon_count))
    return (rebuilt, feat_grad, enc_sum * norm_scale, gen_sum * norm_scale)


def solution(mesh):
    return jax.shard_map(
        on_device,
        mesh=mesh,
        in_specs=(P(None, "lat", "lon"), P(), P(), P(None, "lat", "lon")),
        out_specs=(P(None, "lat", "lon"), P(None, "lat", "lon"), P(), P()),
        check_vma=False,
    )
```

profile of v0, /device:TPU:0, one launch (start us, length us, event | category | flops | bytes accessed | tf_op | source)
XLA Modules:
  0.0 219.3 jit_solution(15706340045346851141)
XLA Ops:
  8.3 1.1 copy.91
  10.1 2.4 %collective-permute-start.1 = (bf16[138,16,1]{0,1,2:T(8,128)(2,1)S(1)}, bf16[138,16,1]{0,1,2:T(8,128)(2,1)S(1)}, u32[]{:S(2)}, u32[]{:S(2)}) collective-permute-start(bf16[138,16,1]{0,1,2:T(8,128)(2,1)S(1)} %copy.93), channel_id=1, source_target_pairs={{1,0},{2,1},{3,2},{0,3},{5,4},{6,5},{7,6},{4,7},{9,8},{10,9},{11,1... | collective-permute-start | bytes 13256 | tf_op jit(solution)/shard_map/ppermute | solution.py:17
  14.3 1.8 collective-permute-done
  17.5 1.3 collective-permute-start.4
  18.8 4.7 %collective-permute-start.3 = (bf16[138,1,130]{2,0,1:T(8,128)(2,1)S(1)}, bf16[138,1,130]{2,0,1:T(8,128)(2,1)S(1)}, u32[]{:S(2)}, u32[]{:S(2)}) collective-permute-start(bf16[138,1,130]{2,0,1:T(8,128)(2,1)S(1)} %get-tuple-element.52), channel_id=1, source_target_pairs={{0,4},{4,8},{8,12},{12,16},{16,20},{20,24},{24,28},{1,5},{5,9},{9,... | collective-permute-start | bytes 107648 | tf_op jit(solution)/shard_map/ppermute | solution.py:15
  39.2 1.5 fusion.23
  47.0 1.7 collective-permute-start.6
  49.7 1.8 copy.144
  51.5 4.4 %collective-permute-start.8 = (bf16[256,1,130]{0,2,1:T(8,128)(2,1)S(1)}, bf16[256,1,130]{0,2,1:T(8,128)(2,1)S(1)}, u32[]{:S(2)}, u32[]{:S(2)}) collective-permute-start(bf16[256,1,130]{0,2,1:T(8,128)(2,1)S(1)} %get-tuple-element.65), channel_id=1, source_target_pairs={{0,4},{4,8},{8,12},{12,16},{16,20},{20,24},{24,28},{1,5},{5,9},{9,... | collective-permute-start | bytes 199688 | tf_op jit(solution)/shard_map/ppermute | solution.py:15
  55.9 1.3 collective-permute-start.9
  57.2 1.5 collective-permute-start.7
  60.0 3.3 %collective-permute-done.9 = bf16[256,1,130]{0,2,1:T(8,128)(2,1)S(1)} collective-permute-done((bf16[256,1,130]{0,2,1:T(8,128)(2,1)S(1)}, bf16[256,1,130]{0,2,1:T(8,128)(2,1)S(1)}, u32[]{:S(2)}, u32[]{:S(2)}) %collective-permute-start.9) | collective-permute-done | bytes 66592 | tf_op jit(solution)/shard_map/ppermute | solution.py:17
  66.1 3.3 %fusion.119 = (bf16[256,16,128]{0,2,1:T(8,128)(2,1)}, bf16[256,16,128]{0,2,1:T(8,128)(2,1)S(1)}, bf16[256,16,128]{0,2,1:T(8,128)(2,1)S(1)}, bf16[256,16,128]{0,2...) fusion(bf16[256,17,130]{0,2,1:T(8,128)(2,1)S(1)} %get-tuple-element.64, ...), kind=kLoop, calls=%fused_computation.229 | loop fusion | bytes 12582912 | tf_op jit(solution)/shard_map/slice | solution.py:52
  69.4 2.0 fusion.38
  71.4 2.0 fusion.57
  74.4 2.0 convolution_add_fusion.13
  76.4 1.3 convolution_add_fusion.12
  77.7 1.2 fusion.10
  79.0 1.3 fusion.11
  80.3 1.2 convolution_add_fusion.9
  81.5 1.2 fusion.12
  83.5 125.0 %all-reduce.3.cloned.1.call-done = (f32[3,3,256,69]{2,3,1,0:T(8,128)}, f32[3,3,69,256]{3,2,1,0:T(8,128)}) async-done(((f32[3,3,256,69]{2,3,1,0:T(8,128)}, f32[3,3,69,256]{3,2,1,0:T(8,128)}), (f32[3,3,256,69]{2,3,1,0:T(8,128)}, f32[3,3,69,256]{3,2,1,0:T(8,128)})) %all-reduce.3.cloned.1.call-update) | async-done | bytes 1271824 | tf_op jit(solution)/shard_map/psum | solution.py:113
  208.5 2.0 broadcast_multiply_fusion.1
  210.5 2.0 broadcast_multiply_fusion
  (154 shorter events, 33.0 us)
Async XLA Ops:
  7.2 5.8 %copy-start.3 = (bf16[69,16,128]{2,1,0:T(8,128)(2,1)S(1)}, bf16[69,16,128]{2,1,0:T(8,128)(2,1)}, u32[]{:S(2)}) copy-start(bf16[69,16,128]{2,1,0:T(8,128)(2,1)} %param.8) | copy-start | bytes 847876
  7.2 201.4 %all-reduce.3.cloned.1.call-start = ((), (), s32[]{:S(2)}) async-start(), calls=%async_computation | async-start | bytes 2654208 | tf_op jit(solution)/shard_map/psum | solution.py:113
  8.3 4.7 %copy-start = (bf16[69,16,128]{2,1,0:T(8,128)(2,1)S(1)}, bf16[69,16,128]{2,1,0:T(8,128)(2,1)}, u32[]{:S(2)}) copy-start(bf16[69,16,128]{2,1,0:T(8,128)(2,1)} %param.11) | copy-start | bytes 847876
  10.1 3.8 %collective-permute-start.1 = (bf16[138,16,1]{0,1,2:T(8,128)(2,1)S(1)}, bf16[138,16,1]{0,1,2:T(8,128)(2,1)S(1)}, u32[]{:S(2)}, u32[]{:S(2)}) collective-permute-start(bf16[138,16,1]{0,1,2:T(8,128)(2,1)S(1)} %copy.93), channel_id=1, source_target_pairs={{1,0},{2,1},{3,2},{0,3},{5,4},{6,5},{7,6},{4,7},{9,8},{10,9},{11,1... | collective-permute-start | bytes 13256 | tf_op jit(solution)/shard_map/ppermute | solution.py:17
  12.9 3.1 %collective-permute-start = (bf16[138,16,1]{0,1,2:T(8,128)(2,1)S(1)}, bf16[138,16,1]{0,1,2:T(8,128)(2,1)S(1)}, u32[]{:S(2)}, u32[]{:S(2)}) collective-permute-start(bf16[138,16,1]{0,1,2:T(8,128)(2,1)S(1)} %copy.92), channel_id=1, source_target_pairs={{0,1},{1,2},{2,3},{3,0},{4,5},{5,6},{6,7},{7,4},{8,9},{9,10},{10,1... | collective-permute-start | bytes 13256 | tf_op jit(solution)/shard_map/ppermute | solution.py:15
  17.5 7.0 %collective-permute-start.4 = (bf16[138,1,130]{2,0,1:T(8,128)(2,1)S(1)}, bf16[138,1,130]{2,0,1:T(8,128)(2,1)S(1)}, u32[]{:S(2)}, u32[]{:S(2)}) collective-permute-start(bf16[138,1,130]{2,0,1:T(8,128)(2,1)S(1)} %get-tuple-element.51), channel_id=1, source_target_pairs={{4,0},{8,4},{12,8},{16,12},{20,16},{24,20},{28,24},{5,1},{9,5},{13... | collective-permute-start | bytes 107648 | tf_op jit(solution)/shard_map/ppermute | solution.py:17
  18.8 6.6 %collective-permute-start.3 = (bf16[138,1,130]{2,0,1:T(8,128)(2,1)S(1)}, bf16[138,1,130]{2,0,1:T(8,128)(2,1)S(1)}, u32[]{:S(2)}, u32[]{:S(2)}) collective-permute-start(bf16[138,1,130]{2,0,1:T(8,128)(2,1)S(1)} %get-tuple-element.52), channel_id=1, source_target_pairs={{0,4},{4,8},{8,12},{12,16},{16,20},{20,24},{24,28},{1,5},{5,9},{9,... | collective-permute-start | bytes 107648 | tf_op jit(solution)/shard_map/ppermute | solution.py:15
  23.5 9.0 %collective-permute-start.2 = (bf16[138,2,130]{2,0,1:T(8,128)(2,1)S(1)}, bf16[138,2,130]{2,0,1:T(8,128)(2,1)S(1)}, u32[]{:S(2)}, u32[]{:S(2)}) collective-permute-start(bf16[138,2,130]{2,0,1:T(8,128)(2,1)S(1)} %pad_maximum_fusion.29), channel_id=1, source_target_pairs={{0,2},{1,3},{2,0},{3,1},{4,6},{5,7},{6,4},{7,5},{8,10},{9,11},{10,... | collective-permute-start | bytes 215288 | tf_op jit(solution)/shard_map/ppermute | solution.py:27
  27.0 1.0 copy-start.6
  33.6 1.0 copy-start.8
  45.1 1.5 copy-start.4
  46.9 4.5 %collective-permute-start.5 = (bf16[256,16,1]{0,2,1:T(2,128)(2,1)}, bf16[256,16,1]{0,2,1:T(2,128)(2,1)S(1)}, u32[]{:S(2)}, u32[]{:S(2)}) collective-permute-start(bf16[256,16,1]{0,2,1:T(2,128)(2,1)} %get-tuple-element.69), channel_id=1, source_target_pairs={{0,1},{1,2},{2,3},{3,0},{4,5},{5,6},{6,7},{7,4},{8,9},{9,10},{10,1... | collective-permute-start | bytes 24584 | tf_op jit(solution)/shard_map/ppermute | solution.py:15
  47.0 4.5 %collective-permute-start.6 = (bf16[256,16,1]{0,2,1:T(2,128)(2,1)S(1)}, bf16[256,16,1]{0,2,1:T(2,128)(2,1)S(1)}, u32[]{:S(2)}, u32[]{:S(2)}) collective-permute-start(bf16[256,16,1]{0,2,1:T(2,128)(2,1)S(1)} %get-tuple-element.70), channel_id=1, source_target_pairs={{1,0},{2,1},{3,2},{0,3},{5,4},{6,5},{7,6},{4,7},{9,8},{10,9},{11,1... | collective-permute-start | bytes 24584 | tf_op jit(solution)/shard_map/ppermute | solution.py:17
  51.5 8.4 %collective-permute-start.8 = (bf16[256,1,130]{0,2,1:T(8,128)(2,1)S(1)}, bf16[256,1,130]{0,2,1:T(8,128)(2,1)S(1)}, u32[]{:S(2)}, u32[]{:S(2)}) collective-permute-start(bf16[256,1,130]{0,2,1:T(8,128)(2,1)S(1)} %get-tuple-element.65), channel_id=1, source_target_pairs={{0,4},{4,8},{8,12},{12,16},{16,20},{20,24},{24,28},{1,5},{5,9},{9,... | collective-permute-start | bytes 199688 | tf_op jit(solution)/shard_map/ppermute | solution.py:15
  55.9 7.3 %collective-permute-start.9 = (bf16[256,1,130]{0,2,1:T(8,128)(2,1)S(1)}, bf16[256,1,130]{0,2,1:T(8,128)(2,1)S(1)}, u32[]{:S(2)}, u32[]{:S(2)}) collective-permute-start(bf16[256,1,130]{0,2,1:T(8,128)(2,1)S(1)} %get-tuple-element.66), channel_id=1, source_target_pairs={{4,0},{8,4},{12,8},{16,12},{20,16},{24,20},{28,24},{5,1},{9,5},{13... | collective-permute-start | bytes 199688 | tf_op jit(solution)/shard_map/ppermute | solution.py:17
  57.2 6.0 %collective-permute-start.7 = (bf16[256,2,130]{0,2,1:T(8,128)(2,1)S(1)}, bf16[256,2,130]{0,2,1:T(8,128)(2,1)S(1)}, u32[]{:S(2)}, u32[]{:S(2)}) collective-permute-start(bf16[256,2,130]{0,2,1:T(8,128)(2,1)S(1)} %pad_maximum_fusion.30), channel_id=1, source_target_pairs={{0,2},{1,3},{2,0},{3,1},{4,6},{5,7},{6,4},{7,5},{8,10},{9,11},{10,... | collective-permute-start | bytes 399368 | tf_op jit(solution)/shard_map/ppermute | solution.py:27
  74.4 2.0 copy-start.1
  74.4 3.3 %copy-start.7 = (f32[2048,69]{0,1:T(8,128)S(1)}, f32[2048,69]{0,1:T(8,128)}, u32[]{:S(2)}) copy-start(f32[2048,69]{0,1:T(8,128)} %fusion.23) | copy-start | bytes 1695748
  76.4 2.5 %copy-start.5 = (f32[2048,69]{0,1:T(8,128)S(1)}, f32[2048,69]{0,1:T(8,128)}, u32[]{:S(2)}) copy-start(f32[2048,69]{0,1:T(8,128)} %fusion.38) | copy-start | bytes 1695748
  78.9 2.5 %copy-start.2 = (bf16[256,16,128]{0,2,1:T(8,128)(2,1)S(1)}, bf16[256,16,128]{0,2,1:T(8,128)(2,1)}, u32[]{:S(2)}) copy-start(bf16[256,16,128]{0,2,1:T(8,128)(2,1)} %get-tuple-element.53) | copy-start | bytes 3145732
Sparse Core Ops, SparseCore 0:
  74.5 133.9 all-reduce.2
where the time goes:
time: 220 us; the launch traced here: 219 us
  waiting for transfers between devices  131 us (60%)
  matrix products  30 us (14%)
  starting transfers between devices  18.1 us (8%)
  between operations  15 us (7%)
  local copies, waits for them, and re-layouts  13.7 us (6%)
  other arithmetic  11.7 us (5%)
    psum x1, waiting for transfers between devices, sum_grads(): summed = lax.psum((enc_part, gen_part), ('lat', 'lon'))  125 us
    dot_general x18, matrix products, convolve(): jnp.dot(kernel[row_tap, col_tap], section, preferred_element_type=jnp.flo...  18.4 us
    ppermute x4, starting transfers between devices, extended(): lax.ppermute(tail, axis, [(i, (i + 1) % count) for i in range(ends)])  9.17 us
    unnamed x58, local copies, waits for them, and re-layouts  6.96 us
    ppermute x4, starting transfers between devices, extended(): lax.ppermute(head, axis, [((i + 1) % count, i) for i in range(ends)])  6.75 us
    dot_general x18, matrix products, weight_grad(): lax.dot_general(flat_cot, section, (((1,), (1,)), ((), ())), preferred_el...  5.67 us
  transfers between devices with their start and end apart: 11, of which 4 were waited for; matrix products, arithmetic and copies ran while one was open for 10% of the time, Pallas kernels for 0%

commit v1 on v0

--- a/solution.py
+++ b/solution.py
@@ -110,7 +110,7 @@
 
 
 def sum_grads(enc_part, gen_part):
-    summed = lax.psum((enc_part, gen_part), ("lat", "lon"))
+    summed = lax.psum(lax.psum((enc_part, gen_part), "lon"), "lat")
     return summed
 
 

time: 220 us -> 212 us (0.964)
  waiting for transfers between devices: 131 us -> 122 us
    psum x1 -> x2, waiting for transfers between devices: 125 us -> 116 us  [sum_grads(): summed = lax.psum(lax.psum((enc_part, gen_part), 'lon'), 'lat')]
    unnamed x58 -> x54, local copies, waits for them, and re-layouts: 6.96 us -> 6.95 us
  transfers between devices with their start and end apart: 11 -> 12, of which waited for: 4 -> 5; matrix products, arithmetic and copies ran while one was open for 10% -> 12% of each run, Pallas kernels for 0% -> 0%
where the time goes in v1:
time: 212 us; the launch traced here: 211 us
  waiting for transfers between devices  122 us (58%)
  matrix products  30.3 us (14%)
  starting transfers between devices  18.2 us (9%)
  between operations  15 us (7%)
  local copies, waits for them, and re-layouts  14.3 us (7%)
  other arithmetic  11.7 us (6%)
    psum x2, waiting for transfers between devices, sum_grads(): summed = lax.psum(lax.psum((enc_part, gen_part), 'lon'), 'lat')  116 us
    dot_general x18, matrix products, convolve(): jnp.dot(kernel[row_tap, col_tap], section, preferred_element_type=jnp.flo...  18.7 us
    ppermute x4, starting transfers between devices, extended(): lax.ppermute(tail, axis, [(i, (i + 1) % count) for i in range(ends)])  9.17 us
    unnamed x54, local copies, waits for them, and re-layouts  6.95 us
    ppermute x4, starting transfers between devices, extended(): lax.ppermute(head, axis, [((i + 1) % count, i) for i in range(ends)])  6.75 us
    dot_general x18, matrix products, weight_grad(): lax.dot_general(flat_cot, section, (((1,), (1,)), ((), ())), preferred_el...  5.66 us
    dot_general x9, matrix products, adjoint_conv(): lax.dot_general(kernel[row_tap, col_tap], section, (((0,), (0,)), ((), ()...  4.37 us
  transfers between devices with their start and end apart: 12, of which 5 were waited for; matrix products, arithmetic and copies ran while one was open for 12% of the time, Pallas kernels for 0%

profile of v1, /device:TPU:0, one launch (start us, length us, event | category | flops | bytes accessed | tf_op | source)
XLA Modules:
  0.0 211.2 jit_solution(4105708106610237733)
XLA Ops:
  10.1 2.4 %collective-permute-start.1 = (bf16[138,16,1]{0,1,2:T(8,128)(2,1)S(1)}, bf16[138,16,1]{0,1,2:T(8,128)(2,1)S(1)}, u32[]{:S(2)}, u32[]{:S(2)}) collective-permute-start(bf16[138,16,1]{0,1,2:T(8,128)(2,1)S(1)} %copy.93), channel_id=1, source_target_pairs={{1,0},{2,1},{3,2},{0,3},{5,4},{6,5},{7,6},{4,7},{9,8},{10,9},{11,1... | collective-permute-start | bytes 13256 | tf_op jit(solution)/shard_map/ppermute | solution.py:17
  14.3 1.8 collective-permute-done
  17.5 1.3 collective-permute-start.4
  18.8 4.7 %collective-permute-start.3 = (bf16[138,1,130]{2,0,1:T(8,128)(2,1)S(1)}, bf16[138,1,130]{2,0,1:T(8,128)(2,1)S(1)}, u32[]{:S(2)}, u32[]{:S(2)}) collective-permute-start(bf16[138,1,130]{2,0,1:T(8,128)(2,1)S(1)} %get-tuple-element.54), channel_id=1, source_target_pairs={{0,4},{4,8},{8,12},{12,16},{16,20},{20,24},{24,28},{1,5},{5,9},{9,... | collective-permute-start | bytes 107648 | tf_op jit(solution)/shard_map/ppermute | solution.py:15
  39.2 1.5 fusion.23
  47.0 1.7 collective-permute-start.6
  49.7 1.8 copy.144
  51.5 4.4 %collective-permute-start.8 = (bf16[256,1,130]{0,2,1:T(8,128)(2,1)S(1)}, bf16[256,1,130]{0,2,1:T(8,128)(2,1)S(1)}, u32[]{:S(2)}, u32[]{:S(2)}) collective-permute-start(bf16[256,1,130]{0,2,1:T(8,128)(2,1)S(1)} %get-tuple-element.67), channel_id=1, source_target_pairs={{0,4},{4,8},{8,12},{12,16},{16,20},{20,24},{24,28},{1,5},{5,9},{9,... | collective-permute-start | bytes 199688 | tf_op jit(solution)/shard_map/ppermute | solution.py:15
  55.9 1.3 collective-permute-start.9
  57.2 1.5 collective-permute-start.7
  60.0 3.3 %collective-permute-done.9 = bf16[256,1,130]{0,2,1:T(8,128)(2,1)S(1)} collective-permute-done((bf16[256,1,130]{0,2,1:T(8,128)(2,1)S(1)}, bf16[256,1,130]{0,2,1:T(8,128)(2,1)S(1)}, u32[]{:S(2)}, u32[]{:S(2)}) %collective-permute-start.9) | collective-permute-done | bytes 66592 | tf_op jit(solution)/shard_map/ppermute | solution.py:17
  66.1 3.9 %fusion.119 = (bf16[256,16,128]{0,2,1:T(8,128)(2,1)}, bf16[256,16,128]{0,2,1:T(8,128)(2,1)S(1)}, bf16[256,16,128]{0,2,1:T(8,128)(2,1)}, bf16[256,16,128]{0,2,1:T...) fusion(bf16[256,17,130]{0,2,1:T(8,128)(2,1)S(1)} %get-tuple-element.66, ...), kind=kLoop, calls=%fused_computation.229 | loop fusion | bytes 12582912 | tf_op jit(solution)/shard_map/slice | solution.py:52
  71.0 1.7 fusion.57
  72.8 1.7 convolution_add_fusion.13
  74.5 2.0 convolution_add_fusion.12
  76.5 36.5 %all-reduce.7.cloned.1.call-done = (f32[3,3,256,69]{2,3,1,0:T(8,128)}, f32[3,3,69,256]{3,2,1,0:T(8,128)}) async-done(((f32[3,3,256,69]{2,3,1,0:T(8,128)}, f32[3,3,69,256]{3,2,1,0:T(8,128)}), (f32[3,3,256,69]{2,3,1,0:T(8,128)}, f32[3,3,69,256]{3,2,1,0:T(8,128)})) %all-reduce.7.cloned.1.call-update) | async-done | bytes 1271824 | tf_op jit(solution)/shard_map/psum | solution.py:113
  113.0 1.7 fusion.38
  114.7 1.7 fusion.10
  116.4 1.3 fusion.11
  117.7 1.2 convolution_add_fusion.9
  118.9 1.2 fusion.12
  120.9 79.4 %all-reduce.5.cloned.1.call-done = (f32[3,3,256,69]{2,3,1,0:T(8,128)}, f32[3,3,69,256]{3,2,1,0:T(8,128)}) async-done(((f32[3,3,256,69]{2,3,1,0:T(8,128)}, f32[3,3,69,256]{3,2,1,0:T(8,128)}), (f32[3,3,256,69]{2,3,1,0:T(8,128)}, f32[3,3,69,256]{3,2,1,0:T(8,128)})) %all-reduce.5.cloned.1.call-update) | async-done | bytes 1271824 | tf_op jit(solution)/shard_map/psum | solution.py:113
  200.4 2.0 broadcast_multiply_fusion.1
  202.4 2.0 broadcast_multiply_fusion
  (153 shorter events, 34.2 us)
Async XLA Ops:
  7.2 5.8 %copy-start.3 = (bf16[69,16,128]{2,1,0:T(8,128)(2,1)S(1)}, bf16[69,16,128]{2,1,0:T(8,128)(2,1)}, u32[]{:S(2)}) copy-start(bf16[69,16,128]{2,1,0:T(8,128)(2,1)} %param.8) | copy-start | bytes 847876
  7.2 105.8 %all-reduce.7.cloned.1.call-start = ((), (), s32[]{:S(2)}) async-start(), calls=%async_computation.1 | async-start | bytes 2654208 | tf_op jit(solution)/shard_map/psum | solution.py:113
  8.3 4.7 %copy-start = (bf16[69,16,128]{2,1,0:T(8,128)(2,1)S(1)}, bf16[69,16,128]{2,1,0:T(8,128)(2,1)}, u32[]{:S(2)}) copy-start(bf16[69,16,128]{2,1,0:T(8,128)(2,1)} %param.11) | copy-start | bytes 847876
  10.1 3.8 %collective-permute-start.1 = (bf16[138,16,1]{0,1,2:T(8,128)(2,1)S(1)}, bf16[138,16,1]{0,1,2:T(8,128)(2,1)S(1)}, u32[]{:S(2)}, u32[]{:S(2)}) collective-permute-start(bf16[138,16,1]{0,1,2:T(8,128)(2,1)S(1)} %copy.93), channel_id=1, source_target_pairs={{1,0},{2,1},{3,2},{0,3},{5,4},{6,5},{7,6},{4,7},{9,8},{10,9},{11,1... | collective-permute-start | bytes 13256 | tf_op jit(solution)/shard_map/ppermute | solution.py:17
  12.9 3.1 %collective-permute-start = (bf16[138,16,1]{0,1,2:T(8,128)(2,1)S(1)}, bf16[138,16,1]{0,1,2:T(8,128)(2,1)S(1)}, u32[]{:S(2)}, u32[]{:S(2)}) collective-permute-start(bf16[138,16,1]{0,1,2:T(8,128)(2,1)S(1)} %copy.92), channel_id=1, source_target_pairs={{0,1},{1,2},{2,3},{3,0},{4,5},{5,6},{6,7},{7,4},{8,9},{9,10},{10,1... | collective-permute-start | bytes 13256 | tf_op jit(solution)/shard_map/ppermute | solution.py:15
  17.5 7.0 %collective-permute-start.4 = (bf16[138,1,130]{2,0,1:T(8,128)(2,1)S(1)}, bf16[138,1,130]{2,0,1:T(8,128)(2,1)S(1)}, u32[]{:S(2)}, u32[]{:S(2)}) collective-permute-start(bf16[138,1,130]{2,0,1:T(8,128)(2,1)S(1)} %get-tuple-element.53), channel_id=1, source_target_pairs={{4,0},{8,4},{12,8},{16,12},{20,16},{24,20},{28,24},{5,1},{9,5},{13... | collective-permute-start | bytes 107648 | tf_op jit(solution)/shard_map/ppermute | solution.py:17
  18.8 6.6 %collective-permute-start.3 = (bf16[138,1,130]{2,0,1:T(8,128)(2,1)S(1)}, bf16[138,1,130]{2,0,1:T(8,128)(2,1)S(1)}, u32[]{:S(2)}, u32[]{:S(2)}) collective-permute-start(bf16[138,1,130]{2,0,1:T(8,128)(2,1)S(1)} %get-tuple-element.54), channel_id=1, source_target_pairs={{0,4},{4,8},{8,12},{12,16},{16,20},{20,24},{24,28},{1,5},{5,9},{9,... | collective-permute-start | bytes 107648 | tf_op jit(solution)/shard_map/ppermute | solution.py:15
  23.5 9.0 %collective-permute-start.2 = (bf16[138,2,130]{2,0,1:T(8,128)(2,1)S(1)}, bf16[138,2,130]{2,0,1:T(8,128)(2,1)S(1)}, u32[]{:S(2)}, u32[]{:S(2)}) collective-permute-start(bf16[138,2,130]{2,0,1:T(8,128)(2,1)S(1)} %pad_maximum_fusion.29), channel_id=1, source_target_pairs={{0,2},{1,3},{2,0},{3,1},{4,6},{5,7},{6,4},{7,5},{8,10},{9,11},{10,... | collective-permute-start | bytes 215288 | tf_op jit(solution)/shard_map/ppermute | solution.py:27
  27.0 1.0 copy-start.5
  33.6 1.0 copy-start.6
  45.1 1.5 copy-start.4
  46.9 4.5 %collective-permute-start.5 = (bf16[256,16,1]{0,2,1:T(2,128)(2,1)}, bf16[256,16,1]{0,2,1:T(2,128)(2,1)S(1)}, u32[]{:S(2)}, u32[]{:S(2)}) collective-permute-start(bf16[256,16,1]{0,2,1:T(2,128)(2,1)} %get-tuple-element.71), channel_id=1, source_target_pairs={{0,1},{1,2},{2,3},{3,0},{4,5},{5,6},{6,7},{7,4},{8,9},{9,10},{10,1... | collective-permute-start | bytes 24584 | tf_op jit(solution)/shard_map/ppermute | solution.py:15
  47.0 4.5 %collective-permute-start.6 = (bf16[256,16,1]{0,2,1:T(2,128)(2,1)S(1)}, bf16[256,16,1]{0,2,1:T(2,128)(2,1)S(1)}, u32[]{:S(2)}, u32[]{:S(2)}) collective-permute-start(bf16[256,16,1]{0,2,1:T(2,128)(2,1)S(1)} %get-tuple-element.72), channel_id=1, source_target_pairs={{1,0},{2,1},{3,2},{0,3},{5,4},{6,5},{7,6},{4,7},{9,8},{10,9},{11,1... | collective-permute-start | bytes 24584 | tf_op jit(solution)/shard_map/ppermute | solution.py:17
  51.5 8.4 %collective-permute-start.8 = (bf16[256,1,130]{0,2,1:T(8,128)(2,1)S(1)}, bf16[256,1,130]{0,2,1:T(8,128)(2,1)S(1)}, u32[]{:S(2)}, u32[]{:S(2)}) collective-permute-start(bf16[256,1,130]{0,2,1:T(8,128)(2,1)S(1)} %get-tuple-element.67), channel_id=1, source_target_pairs={{0,4},{4,8},{8,12},{12,16},{16,20},{20,24},{24,28},{1,5},{5,9},{9,... | collective-permute-start | bytes 199688 | tf_op jit(solution)/shard_map/ppermute | solution.py:15
  55.9 7.3 %collective-permute-start.9 = (bf16[256,1,130]{0,2,1:T(8,128)(2,1)S(1)}, bf16[256,1,130]{0,2,1:T(8,128)(2,1)S(1)}, u32[]{:S(2)}, u32[]{:S(2)}) collective-permute-start(bf16[256,1,130]{0,2,1:T(8,128)(2,1)S(1)} %get-tuple-element.68), channel_id=1, source_target_pairs={{4,0},{8,4},{12,8},{16,12},{20,16},{24,20},{28,24},{5,1},{9,5},{13... | collective-permute-start | bytes 199688 | tf_op jit(solution)/shard_map/ppermute | solution.py:17
  57.2 6.0 %collective-permute-start.7 = (bf16[256,2,130]{0,2,1:T(8,128)(2,1)S(1)}, bf16[256,2,130]{0,2,1:T(8,128)(2,1)S(1)}, u32[]{:S(2)}, u32[]{:S(2)}) collective-permute-start(bf16[256,2,130]{0,2,1:T(8,128)(2,1)S(1)} %pad_maximum_fusion.30), channel_id=1, source_target_pairs={{0,2},{1,3},{2,0},{3,1},{4,6},{5,7},{6,4},{7,5},{8,10},{9,11},{10,... | collective-permute-start | bytes 399368 | tf_op jit(solution)/shard_map/ppermute | solution.py:27
  71.0 129.4 %all-reduce.5.cloned.1.call-start = ((), (), s32[]{:S(2)}) async-start(), calls=%async_computation | async-start | bytes 2654208 | tf_op jit(solution)/shard_map/psum | solution.py:113
  71.0 3.4 %copy-start.1 = (bf16[256,16,128]{0,2,1:T(8,128)(2,1)S(1)}, bf16[256,16,128]{0,2,1:T(8,128)(2,1)}, u32[]{:S(2)}) copy-start(bf16[256,16,128]{0,2,1:T(8,128)(2,1)} %get-tuple-element.90) | copy-start | bytes 3145732
  116.4 2.5 %copy-start.2 = (bf16[256,16,128]{0,2,1:T(8,128)(2,1)S(1)}, bf16[256,16,128]{0,2,1:T(8,128)(2,1)}, u32[]{:S(2)}) copy-start(bf16[256,16,128]{0,2,1:T(8,128)(2,1)} %get-tuple-element.55) | copy-start | bytes 3145732
Sparse Core Ops, SparseCore 0:
  71.1 41.8 all-reduce.6
  116.6 83.7 all-reduce.4
